TPU v7x, 32 devices: a whole 2x2x4 slice. The times are simulated.
32 devices in a mesh: row: 4 (over x, core), col: 8 (over z, y).
Axes of the slice: x: 2, y: 2, z: 4, core: 2. Of those that a mesh axis runs over, the one named last changes fastest.
Arguments:
- matrix: float32 [2048, 2048], P('row', 'col'), as said below
- panel: float32 [2048, 256], P(('row', 'col')), may hold values from -0.125 to 0.125
- factor: float32 [256, 256], replicated, as said below
Outputs:
- updated: float32 [2048, 2048], P('row', 'col')
- correction: float32 [2048, 256], P(('row', 'col'))
Inputs may be any that keep to these rules, and one draw needn't show every extreme that they name: `matrix`: symmetric. `factor`: upper triangular with a positive diagonal.
All inputs are finite; a program needn't handle non-finite values.
Results may differ from a plain program's by a relative error of at most 0.000071.
Values sent between devices are 32-bit elements; how exact they have to be, the bound alone decides.
A program may use at most 64 MiB of HBM per device.

v0:
```python
import jax
import jax.numpy as jnp
from jax import lax
from jax.sharding import PartitionSpec as P


def from_root(value, axis, source):
    kept = jnp.where(lax.axis_index(axis) == source, value, 0).astype(value.dtype)
    return lax.psum(kept, axis)


def mult(left, right):
    return jnp.dot(left, right, precision=lax.Precision.HIGHEST, preferred_element_type=jnp.float32)


def per_device(matrix, panel, factor):
    ncols = lax.axis_size("col")
    nrows = lax.axis_size("row")
    blocks = panel.shape[0]
    col_index = lax.axis_index("col")
    col_rows = blocks * nrows
    offset = col_index * nrows % ncols * blocks
    owner = col_index * nrows // ncols
    row_panel = lax.all_gather(panel, "col", axis=0, tiled=True)
    col_panel = from_root(lax.dynamic_slice_in_dim(row_panel, offset, col_rows, 0), "row", owner)
    product = lax.psum(mult(matrix, col_panel), "col")
    scaled = mult(product, factor)
    small = lax.psum(mult(row_panel.T, scaled), "row")
    row_corr = scaled - 0.5 * mult(row_panel, mult(factor.T, small))
    correction = lax.dynamic_slice_in_dim(row_corr, col_index * blocks, blocks, 0)
    col_corr = from_root(lax.dynamic_slice_in_dim(row_corr, offset, col_rows, 0), "row", owner)
    updated = matrix - mult(row_panel, col_corr.T) - mult(row_corr, col_panel.T)
    return (updated, correction)


def solution(mesh):
    in_specs = (P("row", "col"), P(("row", "col"), None), P())
    out_specs = (P("row", "col"), P(("row", "col"), None))
    return jax.shard_map(
        per_device, mesh=mesh, in_specs=in_specs, out_specs=out_specs, check_vma=False
    )
```

profile of v0, /device:TPU:0, one launch (start us, length us, event | category | flops | bytes accessed | tf_op | source)
XLA Modules:
  0.0 231.1 jit_solution(12882593466567161444)
XLA Ops:
  7.2 0.0 copy-start
  7.2 0.0 all-reduce.5.cloned.1.call-start
  7.2 33.2 %all_gather.3 = f32[512,256]{1,0:T(8,128)S(1)} all-gather(f32[64,256]{1,0:T(8,128)} %param.4), channel_id=1, replica_groups=mesh['row'=4,'col'=8] {'col'}, dimensions={0}, use_global_device_ids=true | all-gather | bytes 589824 | tf_op jit(solution)/shard_map/all_gather | solution.py:24
  40.5 0.0 copy-start.1
  40.5 0.7 dynamic-slice_select_fusion.1
  41.2 0.0 all-reduce.5.cloned.1.call-update
  41.2 0.0 all-reduce.7.cloned.1.call-start
  41.3 33.5 %all-reduce.5.cloned.1.call-done = f32[256,256]{1,0:T(8,128)} async-done(((f32[256,256]{1,0:T(8,128)}), f32[256,256]{1,0:T(8,128)}) %all-reduce.5.cloned.1.call-update) | async-done | bytes 262160 | tf_op jit(solution)/shard_map/psum | solution.py:9
  74.8 0.0 copy-done.1
  74.8 2.8 %convolution_bitcast_fusion.1 = f32[512,256]{0,1:T(8,128)} fusion(f32[256,256]{1,0:T(8,128)} %all-reduce.5.cloned.1.call-done, f32[512,256]{1,0:T(8,128)S(1)} %copy-done.1), kind=kOutput, calls=%fused_computation.1 | convolution fusion | flops 402653184 | bytes 1310720 | tf_op jit(solution)/shard_map/dot_general | solution.py:13
  77.6 0.0 all-reduce.7.cloned.1.call-update
  77.6 0.0 all-reduce.9.cloned.1.call-start
  77.6 73.8 %all-reduce.7.cloned.1.call-done = f32[512,256]{0,1:T(8,128)} async-done(((f32[512,256]{0,1:T(8,128)}), f32[512,256]{0,1:T(8,128)}) %all-reduce.7.cloned.1.call-update) | async-done | bytes 524304 | tf_op jit(solution)/shard_map/psum | solution.py:26
  151.5 0.0 copy-done
  151.5 2.0 fusion.4
  153.5 1.7 convolution_bitcast_fusion.2
  155.2 0.0 all-reduce.9.cloned.1.call-update
  155.3 0.0 all-reduce.11.cloned.1.call-start
  155.3 0.2 copy.6
  155.5 31.4 %all-reduce.9.cloned.1.call-done = f32[256,256]{0,1:T(8,128)} async-done(((f32[256,256]{0,1:T(8,128)}), f32[256,256]{0,1:T(8,128)}) %all-reduce.9.cloned.1.call-update) | async-done | bytes 262160 | tf_op jit(solution)/shard_map/psum | solution.py:28
  186.9 1.3 fusion.5
  188.2 0.6 fusion.3
  188.8 0.7 dynamic-slice_select_fusion
  189.5 0.0 copy-start.2
  189.6 0.0 all-reduce.11.cloned.1.call-update
  189.6 0.9 copy-done.2
  190.5 0.6 fusion.6
  191.1 0.6 constant_dynamic-slice_fusion
  191.8 30.2 %all-reduce.11.cloned.1.call-done = f32[256,256]{1,0:T(8,128)} async-done(((f32[256,256]{1,0:T(8,128)}), f32[256,256]{1,0:T(8,128)}) %all-reduce.11.cloned.1.call-update) | async-done | bytes 262160 | tf_op jit(solution)/shard_map/psum | solution.py:9
  222.0 1.6 fusion.1
  223.6 1.0 copy.8
Async XLA Ops:
  7.2 144.3 %copy-start = (f32[256,256]{1,0:T(8,128)S(1)}, f32[256,256]{1,0:T(8,128)}, u32[]{:S(2)}) copy-start(f32[256,256]{1,0:T(8,128)} %param.5) | copy-start | bytes 786436
  7.2 67.6 %all-reduce.5.cloned.1.call-start = ((), (), s32[]{:S(2)}) async-start(), calls=%async_computation | async-start | bytes 524288 | tf_op jit(solution)/shard_map/psum | solution.py:9
  40.5 34.3 %copy-start.1 = (f32[512,256]{1,0:T(8,128)S(1)}, f32[512,256]{1,0:T(8,128)}, u32[]{:S(2)}) copy-start(f32[512,256]{1,0:T(8,128)} %param.3) | copy-start | bytes 1572868
  41.2 110.2 %all-reduce.7.cloned.1.call-start = ((), (), s32[]{:S(2)}) async-start(), calls=%async_computation.1 | async-start | bytes 1048576 | tf_op jit(solution)/shard_map/psum | solution.py:26
  77.6 109.3 %all-reduce.9.cloned.1.call-start = ((), (), s32[]{:S(2)}) async-start(), calls=%async_computation.2 | async-start | bytes 524288 | tf_op jit(solution)/shard_map/psum | solution.py:28
  155.3 66.8 %all-reduce.11.cloned.1.call-start = ((), (), s32[]{:S(2)}) async-start(), calls=%async_computation.3 | async-start | bytes 524288 | tf_op jit(solution)/shard_map/psum | solution.py:9
  189.5 0.9 copy-start.2
Sparse Core Ops, SparseCore 0:
  41.4 33.3 all-reduce.4
  78.8 72.6 all-reduce.6
  155.4 31.4 all-reduce.8
  189.7 32.2 all-reduce.10
where the time goes:
time: 231 us
  waiting for transfers between devices  169 us (73%)
  blocking collectives  33.2 us (14%)
  between operations  13.8 us (6%)
  matrix products  10.7 us (5%)
  local copies, waits for them, and re-layouts  2.77 us (1%)
    psum x1, waiting for transfers between devices, per_device(): product = lax.psum(mult(matrix, col_panel), 'col')  73.8 us
    psum x2, waiting for transfers between devices, from_root(): return lax.psum(kept, axis)  63.7 us
    all_gather x1, blocking collectives, per_device(): row_panel = lax.all_gather(panel, 'col', axis=0, tiled=True)  33.2 us
    psum x1, waiting for transfers between devices, per_device(): small = lax.psum(mult(row_panel.T, scaled), 'row')  31.4 us
    dot_general x7, matrix products, mult(): jnp.dot(left, right, precision=lax.Precision.HIGHEST, preferred_element_t...  10.7 us
  transfers between devices with their start and end apart: 4, of which 4 were waited for; matrix products, arithmetic and copies ran while one was open for 1% of the time, Pallas kernels for 0%

commit v1 on v0

--- a/solution.py
+++ b/solution.py
@@ -25,7 +25,7 @@
     col_panel = from_root(lax.dynamic_slice_in_dim(row_panel, offset, col_rows, 0), "row", owner)
     product = lax.psum(mult(matrix, col_panel), "col")
     scaled = mult(product, factor)
-    small = lax.psum(mult(row_panel.T, scaled), "row")
+    small = jnp.sum(lax.all_gather(mult(row_panel.T, scaled), "row"), axis=0)
     row_corr = scaled - 0.5 * mult(row_panel, mult(factor.T, small))
     correction = lax.dynamic_slice_in_dim(row_corr, col_index * blocks, blocks, 0)
     col_corr = from_root(lax.dynamic_slice_in_dim(row_corr, offset, col_rows, 0), "row", owner)

time: 231 us -> 217 us (0.939)
  waiting for transfers between devices: 169 us -> 153 us
    psum x1 -> x0, waiting for transfers between devices: 31.4 us -> none  [per_device(): small = lax.psum(mult(row_panel.T, scaled), 'row')]
    all_gather x0 -> x1, waiting for transfers between devices: none -> 15.8 us  [per_device(): small = jnp.sum(lax.all_gather(mult(row_panel.T, scaled), 'row'), axis=0)]
where the time goes in v1:
time: 217 us
  waiting for transfers between devices  153 us (71%)
  blocking collectives  33.2 us (15%)
  between operations  13.9 us (6%)
  matrix products  9.74 us (4%)
  local copies, waits for them, and re-layouts  4.47 us (2%)
    psum x1, waiting for transfers between devices, per_device(): product = lax.psum(mult(matrix, col_panel), 'col')  73.8 us
    psum x2, waiting for transfers between devices, from_root(): return lax.psum(kept, axis)  63.7 us
    all_gather x1, blocking collectives, per_device(): row_panel = lax.all_gather(panel, 'col', axis=0, tiled=True)  33.2 us
    all_gather x1, waiting for transfers between devices, per_device(): small = jnp.sum(lax.all_gather(mult(row_panel.T, scaled), 'row'), axis=0)  15.8 us
    dot_general x7, matrix products, mult(): jnp.dot(left, right, precision=lax.Precision.HIGHEST, preferred_element_t...  9.74 us
  transfers between devices with their start and end apart: 4, of which 4 were waited for; matrix products, arithmetic and copies ran while one was open for 1% of the time, Pallas kernels for 0%

profile of v1, /device:TPU:0, one launch (start us, length us, event | category | flops | bytes accessed | tf_op | source)
XLA Modules:
  0.0 216.9 jit_solution(10858441932089148347)
XLA Ops:
  7.2 0.0 copy-start
  7.2 0.0 all-reduce.4.cloned.1.call-start
  7.2 33.2 %all_gather.9 = f32[512,256]{1,0:T(8,128)S(1)} all-gather(f32[64,256]{1,0:T(8,128)} %param.4), channel_id=1, replica_groups=mesh['row'=4,'col'=8] {'col'}, dimensions={0}, use_global_device_ids=true | all-gather | bytes 589824 | tf_op jit(solution)/shard_map/all_gather | solution.py:24
  40.5 0.0 copy-start.1
  40.5 0.7 dynamic-slice_select_fusion.1
  41.2 0.0 all-reduce.4.cloned.1.call-update
  41.2 0.0 all-reduce.6.cloned.1.call-start
  41.3 33.5 %all-reduce.4.cloned.1.call-done = f32[256,256]{1,0:T(8,128)} async-done(((f32[256,256]{1,0:T(8,128)}), f32[256,256]{1,0:T(8,128)}) %all-reduce.4.cloned.1.call-update) | async-done | bytes 262160 | tf_op jit(solution)/shard_map/psum | solution.py:9
  74.8 0.0 copy-done.1
  74.8 2.8 %convolution_bitcast_fusion.1 = f32[512,256]{0,1:T(8,128)} fusion(f32[256,256]{1,0:T(8,128)} %all-reduce.4.cloned.1.call-done, f32[512,256]{1,0:T(8,128)S(1)} %copy-done.1), kind=kOutput, calls=%fused_computation.1 | convolution fusion | flops 402653184 | bytes 1310720 | tf_op jit(solution)/shard_map/dot_general | solution.py:13
  77.6 0.0 all-reduce.6.cloned.1.call-update
  77.6 0.0 all-gather.3.cloned.1.call-start
  77.6 73.8 %all-reduce.6.cloned.1.call-done = f32[512,256]{0,1:T(8,128)} async-done(((f32[512,256]{0,1:T(8,128)}), f32[512,256]{0,1:T(8,128)}) %all-reduce.6.cloned.1.call-update) | async-done | bytes 524304 | tf_op jit(solution)/shard_map/psum | solution.py:26
  151.5 0.0 copy-done
  151.5 2.0 fusion.4
  153.5 1.7 convolution_bitcast_fusion.2
  155.2 0.0 all-gather.3.cloned.1.call-update
  155.3 0.0 all-reduce.8.cloned.1.call-start
  155.3 0.2 copy.10
  155.5 15.8 %all-gather.3.cloned.1.call-done = f32[1024,256]{0,1:T(8,128)} async-done(((f32[256,256]{0,1:T(8,128)}), f32[1024,256]{0,1:T(8,128)}) %all-gather.3.cloned.1.call-update) | async-done | bytes 1048592 | tf_op jit(solution)/shard_map/all_gather | solution.py:28
  171.3 1.7 reshape.4
  173.0 0.6 reduce_sum.9
  173.6 0.4 fusion.5
  174.0 0.6 fusion.3
  174.6 0.7 dynamic-slice_select_fusion
  175.4 0.0 all-reduce.8.cloned.1.call-update
  175.4 0.9 copy-done.2
  176.3 0.6 fusion.6
  176.9 0.6 constant_dynamic-slice_fusion
  177.6 30.2 %all-reduce.8.cloned.1.call-done = f32[256,256]{1,0:T(8,128)} async-done(((f32[256,256]{1,0:T(8,128)}), f32[256,256]{1,0:T(8,128)}) %all-reduce.8.cloned.1.call-update) | async-done | bytes 262160 | tf_op jit(solution)/shard_map/psum | solution.py:9
  207.8 1.6 fusion.1
  209.4 1.0 copy.12
  (1 shorter events, 0.0 us)
Async XLA Ops:
  7.2 144.3 %copy-start = (f32[256,256]{1,0:T(8,128)S(1)}, f32[256,256]{1,0:T(8,128)}, u32[]{:S(2)}) copy-start(f32[256,256]{1,0:T(8,128)} %param.5) | copy-start | bytes 786436
  7.2 67.6 %all-reduce.4.cloned.1.call-start = ((), (), s32[]{:S(2)}) async-start(), calls=%async_computation | async-start | bytes 524288 | tf_op jit(solution)/shard_map/psum | solution.py:9
  40.5 34.3 %copy-start.1 = (f32[512,256]{1,0:T(8,128)S(1)}, f32[512,256]{1,0:T(8,128)}, u32[]{:S(2)}) copy-start(f32[512,256]{1,0:T(8,128)} %param.3) | copy-start | bytes 1572868
  41.2 110.2 %all-reduce.6.cloned.1.call-start = ((), (), s32[]{:S(2)}) async-start(), calls=%async_computation.1 | async-start | bytes 1048576 | tf_op jit(solution)/shard_map/psum | solution.py:26
  77.6 93.7 %all-gather.3.cloned.1.call-start = ((), (), s32[]{:S(2)}) async-start(), calls=%async_computation.3 | async-start | bytes 1310720 | tf_op jit(solution)/shard_map/all_gather | solution.py:28
  155.3 52.6 %all-reduce.8.cloned.1.call-start = ((), (), s32[]{:S(2)}) async-start(), calls=%async_computation.2 | async-start | bytes 524288 | tf_op jit(solution)/shard_map/psum | solution.py:9
  175.4 0.9 copy-start.2
Sparse Core Ops, SparseCore 0:
  41.4 33.3 all-reduce.3
  78.8 72.6 all-reduce.5
  155.4 15.8 all-gather.2
  175.5 32.2 all-reduce.7
